TPU v7x, 256 devices: a whole 4x4x8 slice. The times are simulated.
256 devices in a mesh: fsdp: 32 (over z, y_lo, core), tp: 8 (over x, y_hi).
Axes of the slice: x: 4, y: 4 (y_hi: 2, y_lo: 2; y = y_hi * 2 + y_lo), z: 8, core: 2. Of those that a mesh axis runs over, the one named last changes fastest.
Arguments:
- tokens: bfloat16 [2048, 8192], P('tp', 'fsdp'), may hold values from -6 to 6
- gate_blocks: bfloat16 [256, 22, 128, 128], P(('fsdp', 'tp')), may hold values from -0.109375 to 0.109375
- up_blocks: bfloat16 [256, 22, 128, 128], P(('fsdp', 'tp')), may hold values from -0.109375 to 0.109375
- down_blocks: bfloat16 [256, 22, 128, 128], P(('fsdp', 'tp')), may hold values from -0.0546875 to 0.0546875
- gate_index: int32 [256, 22], P('fsdp'), may hold values from 0 to 63, as said below
- up_index: int32 [256, 22], P('fsdp'), may hold values from 0 to 63, as said below
- down_index: int32 [256, 22], P('fsdp'), may hold values from 0 to 63, as said below
- gate_count: int32 [256], P('fsdp'), may hold values from 14 to 22
- up_count: int32 [256], P('fsdp'), may hold values from 14 to 22
- down_count: int32 [256], P('fsdp'), may hold values from 14 to 22
Outputs:
- mixed: bfloat16 [2048, 8192], P('tp', 'fsdp')
Inputs may be any that keep to these rules, and one draw needn't show every extreme that they name: `gate_index`: in each row the first gate_count entries name the kept row blocks of that block column; the 22 entries of a row are different numbers. `up_index`: in each row the first up_count entries name the kept row blocks of that block column; the 22 entries of a row are different numbers. `down_index`: in each row the first down_count entries name the kept column blocks of that block row; the 22 entries of a row are different numbers.
All inputs are finite; a program needn't handle non-finite values.
Results may differ from a plain program's by a relative error of at most 0.0049.
Values may be sent and summed in bfloat16 or wider, within the bound.
No kernel may reach another device: no remote copies, remote signals or barrier semaphores. Data moves between devices by JAX's collectives and lax.ppermute only.
A program may use at most 192 MiB of HBM per device.

v0:
```python
import jax
import jax.numpy as jnp
from jax import lax
from jax.sharding import PartitionSpec as P


def kept_mask(count_part, slot_num):
    return jnp.arange(slot_num, dtype=jnp.int32)[None, :] < count_part[:, None]


def scatter_rows(partial_out):
    return lax.psum_scatter(partial_out, "fsdp", scatter_dimension=1, tiled=True).astype(
        jnp.bfloat16
    )


def body(
    tokens,
    gate_blocks,
    up_blocks,
    down_blocks,
    gate_index,
    up_index,
    down_index,
    gate_count,
    up_count,
    down_count,
):
    whole = lax.all_gather(tokens, "fsdp", axis=1, tiled=True)
    side_len = gate_blocks.shape[-1]
    row_blocks = whole.shape[1] // side_len
    slot_num = gate_index.shape[1]
    block_ids = jnp.arange(row_blocks, dtype=jnp.int32)

    def project_in(block_set, index_part, count_part):
        col_num = index_part.shape[0]
        live_mask = kept_mask(count_part, slot_num)
        onehot = (
            (index_part[:, :, None] == block_ids[None, None, :]) & live_mask[:, :, None]
        ).astype(jnp.bfloat16)
        panel = jnp.einsum("jki,jkcd->icjd", onehot, block_set, preferred_element_type=jnp.bfloat16)
        panel = panel.reshape(row_blocks * side_len, col_num * side_len)
        return jnp.dot(whole, panel, preferred_element_type=jnp.float32)

    pieces = (
        lax.all_gather(gate_blocks, "tp", axis=0, tiled=True),
        lax.all_gather(up_blocks, "tp", axis=0, tiled=True),
    )
    col_num = pieces[0].shape[0]
    gate_part = project_in(pieces[0], gate_index, gate_count)
    up_part = project_in(pieces[1], up_index, up_count)
    hidden = (jax.nn.silu(gate_part) * up_part).astype(jnp.bfloat16)
    piece = lax.all_gather(down_blocks, "tp", axis=0, tiled=True)
    col_num = piece.shape[0]
    index_part = down_index
    count_part = down_count
    live_mask = kept_mask(count_part, slot_num)
    col_num = piece.shape[0]
    live_mask = kept_mask(count_part, slot_num)
    onehot = ((index_part[:, :, None] == block_ids[None, None, :]) & live_mask[:, :, None]).astype(
        jnp.bfloat16
    )
    panel = jnp.einsum("jki,jkcd->jcid", onehot, piece, preferred_element_type=jnp.bfloat16)
    panel = panel.reshape(col_num * side_len, row_blocks * side_len)
    partial_out = jnp.dot(hidden, panel, preferred_element_type=jnp.float32)
    return scatter_rows(partial_out)


def solution(mesh):
    in_specs = (
        P("tp", "fsdp"),
        P(("fsdp", "tp"), None, None, None),
        P(("fsdp", "tp"), None, None, None),
        P(("fsdp", "tp"), None, None, None),
        P("fsdp", None),
        P("fsdp", None),
        P("fsdp", None),
        P("fsdp"),
        P("fsdp"),
        P("fsdp"),
    )
    out_specs = P("tp", "fsdp")
    return jax.shard_map(body, mesh=mesh, in_specs=in_specs, out_specs=out_specs, check_vma=False)
```

profile of v0, /device:TPU:2, one launch (start us, length us, event | category | flops | bytes accessed | tf_op | source)
XLA Modules:
  0.0 527.5 jit_solution(13812759627836743299)
XLA Ops:
  6.5 0.0 all-gather.5.cloned.1.call-start
  6.5 0.7 all-gather.5.cloned.1.call-update
  7.3 0.0 all-gather.9.cloned.1.call-start
  7.3 0.7 all-gather.9.cloned.1.call-update
  8.0 0.0 all-gather.7.cloned.1.call-start
  8.1 0.7 all-gather.7.cloned.1.call-update
  8.7 0.0 all-gather.11.cloned.1.call-start
  8.8 0.5 all-gather.11.cloned.1.call-update
  9.3 0.0 reduce-scatter.2.cloned.1.call-start
  9.4 0.7 iota_compare_fusion.5
  10.1 0.7 iota_compare_fusion.4
  10.8 0.7 iota_compare_fusion.3
  11.5 89.6 %all-gather.5.cloned.1.call-done = bf16[8,22,128,128]{3,2,1,0:T(8,128)(2,1)} async-done(((bf16[1,22,128,128]{3,2,1,0:T(8,128)(2,1)}), bf16[8,22,128,128]{3,2,1,0:T(8,128)(2,1)}) %all-gather.5.cloned.1.call-update) | async-done | bytes 5767184 | tf_op jit(solution)/shard_map/all_gather | solution.py:46
  101.2 14.3 %convolution_bitcast_fusion.1 = bf16[64,128,8,128]{3,0,1,2:T(8,128)(2,1)} fusion(bf16[8,22,128,128]{3,2,1,0:T(8,128)(2,1)} %all-gather.5.cloned.1.call-done, s32[8,22]{1,0:T(8,128)} %param.14, pred[8,22]{1,0:T(8,128)(4,1)S(1)} %iota_compare_fusion.5), kind=kOutput, calls=%fused_computation.10 | convolution fusion | flops 369121280 | bytes 22545264 | tf_op jit(solution)/shard_map/jki,jkcd->icjd/dot_general | solution.py:41
  115.5 0.0 copy-start
  115.5 19.2 %copy.20 = bf16[64,128,8,128]{3,2,1,0:T(8,128)(2,1)} copy(bf16[64,128,8,128]{3,0,1,2:T(8,128)(2,1)} %convolution_bitcast_fusion.1) | data formatting | bytes 33554432 | tf_op jit(solution)/shard_map/jki,jkcd->icjd/transpose | solution.py:41
  134.7 56.4 %all-gather.9.cloned.1.call-done = bf16[8,22,128,128]{3,2,1,0:T(8,128)(2,1)} async-done(((bf16[1,22,128,128]{3,2,1,0:T(8,128)(2,1)}), bf16[8,22,128,128]{3,2,1,0:T(8,128)(2,1)}) %all-gather.9.cloned.1.call-update) | async-done | bytes 5767184 | tf_op jit(solution)/shard_map/all_gather | solution.py:47
  191.2 0.0 copy-done
  191.2 14.1 %convolution_bitcast_fusion = bf16[64,128,8,128]{3,0,1,2:T(8,128)(2,1)} fusion(bf16[8,22,128,128]{3,2,1,0:T(8,128)(2,1)} %all-gather.9.cloned.1.call-done, s32[8,22]{1,0:T(8,128)S(1)} %copy-done, pred[8,22]{1,0:T(8,128)(4,1)S(1)} %iota_compare_fusion.4), kind=kOutput, calls=%fused_computation.9 | convolution fusion | flops 369121280 | bytes 22545264 | tf_op jit(solution)/shard_map/jki,jkcd->icjd/dot_general | solution.py:41
  205.3 18.7 %copy.22 = bf16[64,128,8,128]{3,2,1,0:T(8,128)(2,1)} copy(bf16[64,128,8,128]{3,0,1,2:T(8,128)(2,1)} %convolution_bitcast_fusion) | data formatting | bytes 33554432 | tf_op jit(solution)/shard_map/jki,jkcd->icjd/transpose | solution.py:41
  224.0 40.3 %all-gather.7.cloned.1.call-done = bf16[256,8192]{1,0:T(8,128)(2,1)} async-done(((bf16[256,256]{1,0:T(8,128)(2,1)}), bf16[256,8192]{1,0:T(8,128)(2,1)}) %all-gather.7.cloned.1.call-update) | async-done | bytes 4194320 | tf_op jit(solution)/shard_map/all_gather | solution.py:29
  264.3 0.0 copy-start.2
  264.3 11.8 %fusion.13 = f32[256,1024]{0,1:T(8,128)S(1)} fusion(bf16[256,8192]{1,0:T(8,128)(2,1)} %all-gather.7.cloned.1.call-done, bf16[1024,8,8,128]{3,2,1,0:T(8,128)(2,1)} %bitcast.55), kind=kOutput, calls=%fused_computation.15 | convolution fusion | flops 4294967296 | bytes 22020096 | tf_op jit(solution)/shard_map/dot_general | solution.py:43
  276.1 0.0 copy-done.2
  276.1 0.0 copy-start.1
  276.1 11.4 %fusion.22 = bf16[256,1024]{0,1:T(8,128)(2,1)S(1)} fusion(bf16[256,8192]{1,0:T(8,128)(2,1)S(1)} %copy-done.2, bf16[1024,8,8,128]{3,2,1,0:T(8,128)(2,1)} %bitcast.56, f32[256,1024]{0,1:T(8,128)S(1)} %fusion.13), kind=kOutput, calls=%fused_computation.18 | convolution fusion | flops 4296540160 | bytes 22544384 | tf_op jit(solution)/shard_map/dot_general | solution.py:43
  287.5 66.3 %all-gather.11.cloned.1.call-done = bf16[8,22,128,128]{3,2,1,0:T(8,128)(2,1)} async-done(((bf16[1,22,128,128]{3,2,1,0:T(8,128)(2,1)}), bf16[8,22,128,128]{3,2,1,0:T(8,128)(2,1)}) %all-gather.11.cloned.1.call-update) | async-done | bytes 5767184 | tf_op jit(solution)/shard_map/all_gather | solution.py:53
  353.9 0.0 copy-done.1
  353.9 14.3 %fusion.9 = bf16[8,64,128,128]{3,1,2,0:T(8,128)(2,1)} fusion(bf16[8,22,128,128]{3,2,1,0:T(8,128)(2,1)} %all-gather.11.cloned.1.call-done, s32[8,22]{1,0:T(8,128)S(1)} %copy-done.1, pred[8,22]{1,0:T(8,128)(4,1)S(1)} %iota_compare_fusion.3), kind=kOutput, calls=%fused_computation.11 | convolution fusion | flops 369121280 | bytes 22545264 | tf_op jit(solution)/shard_map/jki,jkcd->jcid/dot_general | solution.py:63
  368.2 20.3 %fusion = f32[256,8192]{1,0:T(8,128)} fusion(bf16[256,1024]{0,1:T(8,128)(2,1)S(1)} %fusion.22, bf16[128,8,64,128]{3,2,1,0:T(8,128)(2,1)} %bitcast.54), kind=kOutput, calls=%fused_computation | convolution fusion | flops 4294967296 | bytes 25690112 | tf_op jit(solution)/shard_map/dot_general | solution.py:65
  388.5 0.0 reduce-scatter.2.cloned.1.call-update
  388.5 130.6 %reduce-scatter.2.cloned.1.call-done = f32[256,256]{1,0:T(8,128)} async-done(((f32[256,8192]{1,0:T(8,128)}), f32[256,256]{1,0:T(8,128)}) %reduce-scatter.2.cloned.1.call-update) | async-done | bytes 262160 | tf_op jit(solution)/shard_map/reduce_scatter | solution.py:12
  519.1 1.6 convert_element_type.10
Async XLA Ops:
  6.5 94.6 %all-gather.5.cloned.1.call-start = ((), (), s32[]{:S(2)}) async-start(), calls=%async_computation.1 | async-start | bytes 6488064 | tf_op jit(solution)/shard_map/all_gather | solution.py:46
  7.3 183.9 %all-gather.9.cloned.1.call-start = ((), (), s32[]{:S(2)}) async-start(), calls=%async_computation.3 | async-start | bytes 6488064 | tf_op jit(solution)/shard_map/all_gather | solution.py:47
  8.0 256.3 %all-gather.7.cloned.1.call-start = ((), (), s32[]{:S(2)}) async-start(), calls=%async_computation.2 | async-start | bytes 4325376 | tf_op jit(solution)/shard_map/all_gather | solution.py:29
  8.7 345.1 %all-gather.11.cloned.1.call-start = ((), (), s32[]{:S(2)}) async-start(), calls=%async_computation.4 | async-start | bytes 6488064 | tf_op jit(solution)/shard_map/all_gather | solution.py:53
  9.3 509.8 %reduce-scatter.2.cloned.1.call-start = ((), (), s32[]{:S(2)}) async-start(), calls=%async_computation.5 | async-start | bytes 8650752 | tf_op jit(solution)/shard_map/reduce_scatter | solution.py:12
  115.5 75.7 %copy-start = (s32[8,22]{1,0:T(8,128)S(1)}, s32[8,22]{1,0:T(8,128)}, u32[]{:S(2)}) copy-start(s32[8,22]{1,0:T(8,128)} %param.15) | copy-start | bytes 2116
  264.3 11.8 %copy-start.2 = (bf16[256,8192]{1,0:T(8,128)(2,1)S(1)}, bf16[256,8192]{1,0:T(8,128)(2,1)}, u32[]{:S(2)}) copy-start(bf16[256,8192]{1,0:T(8,128)(2,1)} %all-gather.7.cloned.1.call-done) | copy-start | bytes 12582916
  276.1 77.8 %copy-start.1 = (s32[8,22]{1,0:T(8,128)S(1)}, s32[8,22]{1,0:T(8,128)}, u32[]{:S(2)}) copy-start(s32[8,22]{1,0:T(8,128)} %param.16) | copy-start | bytes 2116
Sparse Core Ops, SparseCore 0:
  9.9 91.1 all-gather.4
  103.8 87.3 all-gather.8
  192.9 71.2 all-gather.6
  266.7 87.0 all-gather.10
  388.6 130.4 reduce-scatter.1
where the time goes:
time: 533 us; the launch traced here: 528 us
  waiting for transfers between devices  386 us (72%)
  matrix products  86.3 us (16%)
  local copies, waits for them, and re-layouts  38 us (7%)
  between operations  13.4 us (3%)
    reduce_scatter x1, waiting for transfers between devices, scatter_rows(): lax.psum_scatter(partial_out, 'fsdp', scatter_dimension=1, tiled=True)  131 us
    all_gather x1, waiting for transfers between devices, body(): lax.all_gather(gate_blocks, 'tp', axis=0, tiled=True)  89.6 us
    all_gather x1, waiting for transfers between devices, body(): piece = lax.all_gather(down_blocks, 'tp', axis=0, tiled=True)  66.3 us
    all_gather x1, waiting for transfers between devices, body(): lax.all_gather(up_blocks, 'tp', axis=0, tiled=True)  56.4 us
    all_gather x1, waiting for transfers between devices, body(): whole = lax.all_gather(tokens, 'fsdp', axis=1, tiled=True)  40.3 us
    transpose x2, local copies, waits for them, and re-layouts, project_in(): jnp.einsum('jki,jkcd->icjd', onehot, block_set, preferred_element_type=jn...  38 us
    dot_general x2, matrix products, project_in(): jnp.einsum('jki,jkcd->icjd', onehot, block_set, preferred_element_type=jn...  28.4 us
    dot_general x2, matrix products, project_in(): return jnp.dot(whole, panel, preferred_element_type=jnp.float32)  23.2 us
  transfers between devices with their start and end apart: 5, of which 5 were waited for; matrix products, arithmetic and copies ran while one was open for 17% of the time, Pallas kernels for 0%

commit v1 on v0

--- a/solution.py
+++ b/solution.py
@@ -44,7 +44,9 @@
 
     pieces = (
         lax.all_gather(gate_blocks, "tp", axis=0, tiled=True),
-        lax.all_gather(up_blocks, "tp", axis=0, tiled=True),
+        jnp.concatenate(
+            lax.all_to_all(jnp.stack([up_blocks] * lax.axis_size("tp")), "tp", 0, 0), axis=0
+        ),
     )
     col_num = pieces[0].shape[0]
     gate_part = project_in(pieces[0], gate_index, gate_count)

time: 533 us -> 482 us (0.904)
  waiting for transfers between devices: 386 us -> 324 us
  starting transfers between devices: 0.15 us -> 7.69 us
    all_to_all x0 -> x1, waiting for transfers between devices: none -> 93.3 us  [body(): lax.all_to_all(jnp.stack([up_blocks] * lax.axis_size('tp')), 'tp', 0, 0)]
    all_gather x1, waiting for transfers between devices: 89.6 us -> 0.01 us  [body(): lax.all_gather(gate_blocks, 'tp', axis=0, tiled=True)]
    all_gather x1 -> x0, waiting for transfers between devices: 56.4 us -> none  [body(): lax.all_gather(up_blocks, 'tp', axis=0, tiled=True)]
    all_gather x1, waiting for transfers between devices: 40.3 us -> 31.4 us  [body(): whole = lax.all_gather(tokens, 'fsdp', axis=1, tiled=True)]
    all_to_all x0 -> x1, starting transfers between devices: none -> 7.6 us  [body(): lax.all_to_all(jnp.stack([up_blocks] * lax.axis_size('tp')), 'tp', 0, 0)]
  transfers between devices with their start and end apart: 5 -> 5, of which waited for: 5 -> 4; matrix products, arithmetic and copies ran while one was open for 17% -> 20% of each run, Pallas kernels for 0% -> 0%
where the time goes in v1:
time: 482 us; the launch traced here: 476 us
  waiting for transfers between devices  324 us (67%)
  matrix products  86.1 us (18%)
  local copies, waits for them, and re-layouts  42.8 us (9%)
  between operations  13.4 us (3%)
  starting transfers between devices  7.69 us (2%)
    reduce_scatter x1, waiting for transfers between devices, scatter_rows(): lax.psum_scatter(partial_out, 'fsdp', scatter_dimension=1, tiled=True)  131 us
    all_to_all x1, waiting for transfers between devices, body(): lax.all_to_all(jnp.stack([up_blocks] * lax.axis_size('tp')), 'tp', 0, 0)  93.3 us
    all_gather x1, waiting for transfers between devices, body(): piece = lax.all_gather(down_blocks, 'tp', axis=0, tiled=True)  66.5 us
    transpose x2, local copies, waits for them, and re-layouts, project_in(): jnp.einsum('jki,jkcd->icjd', onehot, block_set, preferred_element_type=jn...  37.8 us
    all_gather x1, waiting for transfers between devices, body(): whole = lax.all_gather(tokens, 'fsdp', axis=1, tiled=True)  31.4 us
    dot_general x2, matrix products, project_in(): jnp.einsum('jki,jkcd->icjd', onehot, block_set, preferred_element_type=jn...  28.3 us
    dot_general x2, matrix products, project_in(): return jnp.dot(whole, panel, preferred_element_type=jnp.float32)  23.2 us
    dot_general x1, matrix products, body(): partial_out = jnp.dot(hidden, panel, preferred_element_type=jnp.float32)  20.3 us
  transfers between devices with their start and end apart: 5, of which 4 were waited for; matrix products, arithmetic and copies ran while one was open for 20% of the time, Pallas kernels for 0%

profile of v1, /device:TPU:2, one launch (start us, length us, event | category | flops | bytes accessed | tf_op | source)
XLA Modules:
  0.0 476.0 jit_solution(15092943959855379080)
XLA Ops:
  6.5 0.0 all-gather.4.cloned.1.call-start
  6.5 0.7 all-gather.4.cloned.1.call-update
  7.3 0.0 all-gather.6.cloned.1.call-start
  7.3 0.7 all-gather.6.cloned.1.call-update
  8.0 5.1 %stack.2 = bf16[8,1,22,128,128]{4,3,2,1,0:T(8,128)(2,1)} broadcast(bf16[22,128,128]{2,1,0:T(8,128)(2,1)} %bitcast.61), dimensions={2,3,4} | broadcast | bytes 6488064 | tf_op jit(solution)/shard_map/stack | solution.py:48
  13.1 0.0 copy-start.4
  13.1 0.0 copy-start.5
  13.1 0.0 copy-start.6
  13.1 0.0 copy-start
  13.1 7.6 %all-to-all-start = ((bf16[8,1,22,128,128]{4,3,2,1,0:T(8,128)(2,1)}), bf16[8,1,22,128,128]{4,3,2,1,0:T(8,128)(2,1)}, u32[]{:S(2)}, u32[]{:S(2)}) async-start(bf16[8,1,22,128,128]{4,3,2,1,0:T(8,128)(2,1)} %stack.2), calls=%async_computation | async-start | bytes 11534336 | tf_op jit(solution)/shard_map/all_to_all | solution.py:48
  20.7 0.0 all-gather.8.cloned.1.call-start
  20.7 0.7 all-gather.8.cloned.1.call-update
  21.4 0.0 reduce-scatter.2.cloned.1.call-start
  21.5 0.0 copy-done.4
  21.5 0.1 iota_compare_fusion.5
  21.5 0.0 copy-done.5
  21.5 0.1 iota_compare_fusion.4
  21.6 0.0 copy-done.6
  21.6 0.1 iota_compare_fusion.3
  21.7 93.3 %all-to-all-done = bf16[8,1,22,128,128]{4,3,2,1,0:T(8,128)(2,1)} async-done(((bf16[8,1,22,128,128]{4,3,2,1,0:T(8,128)(2,1)}), bf16[8,1,22,128,128]{4,3,2,1,0:T(8,128)(2,1)}, u32[]{:S(2)}, u32[]{:S(2)}) %all-to-all-start) | async-done | bytes 5767200 | tf_op jit(solution)/shard_map/all_to_all | solution.py:48
  115.0 0.0 copy-done
  115.0 14.2 %convolution_bitcast_fusion = bf16[64,128,8,128]{3,0,1,2:T(8,128)(2,1)} fusion(bf16[8,1,22,128,128]{4,3,2,1,0:T(8,128)(2,1)} %all-to-all-done, s32[8,22]{1,0:T(8,128)S(1)} %copy-done, pred[8,22]{1,0:T(8,128)(4,1)S(1)} %iota_compare_fusion.4), kind=kOutput, calls=%fused_computation.9 | convolution fusion | flops 369121280 | bytes 22545264 | tf_op jit(solution)/shard_map/jki,jkcd->icjd/dot_general | solution.py:41
  129.2 0.0 copy-start.1
  129.2 19.0 %copy.22 = bf16[64,128,8,128]{3,2,1,0:T(8,128)(2,1)} copy(bf16[64,128,8,128]{3,0,1,2:T(8,128)(2,1)} %convolution_bitcast_fusion) | data formatting | bytes 33554432 | tf_op jit(solution)/shard_map/jki,jkcd->icjd/transpose | solution.py:41
  148.2 0.0 all-gather.4.cloned.1.call-done
  148.2 0.0 copy-done.1
  148.2 14.1 %convolution_bitcast_fusion.1 = bf16[64,128,8,128]{3,0,1,2:T(8,128)(2,1)} fusion(bf16[8,22,128,128]{3,2,1,0:T(8,128)(2,1)} %all-gather.4.cloned.1.call-done, s32[8,22]{1,0:T(8,128)S(1)} %copy-done.1, pred[8,22]{1,0:T(8,128)(4,1)S(1)} %iota_compare_fusion.5), kind=kOutput, calls=%fused_computation.10 | convolution fusion | flops 369121280 | bytes 22545264 | tf_op jit(solution)/shard_map/jki,jkcd->icjd/dot_general | solution.py:41
  162.3 18.7 %copy.20 = bf16[64,128,8,128]{3,2,1,0:T(8,128)(2,1)} copy(bf16[64,128,8,128]{3,0,1,2:T(8,128)(2,1)} %convolution_bitcast_fusion.1) | data formatting | bytes 33554432 | tf_op jit(solution)/shard_map/jki,jkcd->icjd/transpose | solution.py:41
  181.1 31.4 %all-gather.6.cloned.1.call-done = bf16[256,8192]{1,0:T(8,128)(2,1)} async-done(((bf16[256,256]{1,0:T(8,128)(2,1)}), bf16[256,8192]{1,0:T(8,128)(2,1)}) %all-gather.6.cloned.1.call-update) | async-done | bytes 4194320 | tf_op jit(solution)/shard_map/all_gather | solution.py:29
  212.5 0.0 copy-start.3
  212.5 11.8 %fusion.14 = f32[256,1024]{0,1:T(8,128)S(1)} fusion(bf16[256,8192]{1,0:T(8,128)(2,1)} %all-gather.6.cloned.1.call-done, bf16[1024,8,8,128]{3,2,1,0:T(8,128)(2,1)} %bitcast.60), kind=kOutput, calls=%fused_computation.16 | convolution fusion | flops 4294967296 | bytes 22020096 | tf_op jit(solution)/shard_map/dot_general | solution.py:43
  224.3 0.0 copy-done.3
  224.3 0.0 copy-start.2
  224.3 11.4 %fusion.23 = bf16[256,1024]{0,1:T(8,128)(2,1)S(1)} fusion(bf16[256,8192]{1,0:T(8,128)(2,1)S(1)} %copy-done.3, bf16[1024,8,8,128]{3,2,1,0:T(8,128)(2,1)} %bitcast.59, f32[256,1024]{0,1:T(8,128)S(1)} %fusion.14), kind=kOutput, calls=%fused_computation.19 | convolution fusion | flops 4296540160 | bytes 22544384 | tf_op jit(solution)/shard_map/dot_general | solution.py:43
  235.8 66.5 %all-gather.8.cloned.1.call-done = bf16[8,22,128,128]{3,2,1,0:T(8,128)(2,1)} async-done(((bf16[1,22,128,128]{3,2,1,0:T(8,128)(2,1)}), bf16[8,22,128,128]{3,2,1,0:T(8,128)(2,1)}) %all-gather.8.cloned.1.call-update) | async-done | bytes 5767184 | tf_op jit(solution)/shard_map/all_gather | solution.py:55
  302.2 0.0 copy-done.2
  302.2 14.3 %fusion.10 = bf16[8,64,128,128]{3,1,2,0:T(8,128)(2,1)} fusion(bf16[8,22,128,128]{3,2,1,0:T(8,128)(2,1)} %all-gather.8.cloned.1.call-done, s32[8,22]{1,0:T(8,128)S(1)} %copy-done.2, pred[8,22]{1,0:T(8,128)(4,1)S(1)} %iota_compare_fusion.3), kind=kOutput, calls=%fused_computation.12 | convolution fusion | flops 369121280 | bytes 22545264 | tf_op jit(solution)/shard_map/jki,jkcd->jcid/dot_general | solution.py:65
  316.6 20.3 %fusion = f32[256,8192]{1,0:T(8,128)} fusion(bf16[256,1024]{0,1:T(8,128)(2,1)S(1)} %fusion.23, bf16[128,8,64,128]{3,2,1,0:T(8,128)(2,1)} %bitcast.58), kind=kOutput, calls=%fused_computation | convolution fusion | flops 4294967296 | bytes 25690112 | tf_op jit(solution)/shard_map/dot_general | solution.py:67
  336.9 0.0 reduce-scatter.2.cloned.1.call-update
  336.9 130.7 %reduce-scatter.2.cloned.1.call-done = f32[256,256]{1,0:T(8,128)} async-done(((f32[256,8192]{1,0:T(8,128)}), f32[256,256]{1,0:T(8,128)}) %reduce-scatter.2.cloned.1.call-update) | async-done | bytes 262160 | tf_op jit(solution)/shard_map/reduce_scatter | solution.py:12
  467.6 1.6 convert_element_type.10
Async XLA Ops:
  6.5 141.7 %all-gather.4.cloned.1.call-start = ((), (), s32[]{:S(2)}) async-start(), calls=%async_computation.2 | async-start | bytes 6488064 | tf_op jit(solution)/shard_map/all_gather | solution.py:46
  7.3 205.3 %all-gather.6.cloned.1.call-start = ((), (), s32[]{:S(2)}) async-start(), calls=%async_computation.3 | async-start | bytes 4325376 | tf_op jit(solution)/shard_map/all_gather | solution.py:29
  13.1 8.4 %copy-start.4 = (s32[8]{0:T(128)S(1)}, s32[8]{0:T(128)}, u32[]{:S(2)}) copy-start(s32[8]{0:T(128)} %param.17) | copy-start | bytes 100
  13.1 8.5 %copy-start.5 = (s32[8]{0:T(128)S(1)}, s32[8]{0:T(128)}, u32[]{:S(2)}) copy-start(s32[8]{0:T(128)} %param.18) | copy-start | bytes 100
  13.1 8.5 %copy-start.6 = (s32[8]{0:T(128)S(1)}, s32[8]{0:T(128)}, u32[]{:S(2)}) copy-start(s32[8]{0:T(128)} %param.19) | copy-start | bytes 100
  13.1 101.9 %copy-start = (s32[8,22]{1,0:T(8,128)S(1)}, s32[8,22]{1,0:T(8,128)}, u32[]{:S(2)}) copy-start(s32[8,22]{1,0:T(8,128)} %param.15) | copy-start | bytes 2116
  13.1 101.9 %all-to-all-start = ((bf16[8,1,22,128,128]{4,3,2,1,0:T(8,128)(2,1)}), bf16[8,1,22,128,128]{4,3,2,1,0:T(8,128)(2,1)}, u32[]{:S(2)}, u32[]{:S(2)}) async-start(bf16[8,1,22,128,128]{4,3,2,1,0:T(8,128)(2,1)} %stack.2), calls=%async_computation | async-start | bytes 11534336 | tf_op jit(solution)/shard_map/all_to_all | solution.py:48
  20.7 281.6 %all-gather.8.cloned.1.call-start = ((), (), s32[]{:S(2)}) async-start(), calls=%async_computation.4 | async-start | bytes 6488064 | tf_op jit(solution)/shard_map/all_gather | solution.py:55
  21.4 446.2 %reduce-scatter.2.cloned.1.call-start = ((), (), s32[]{:S(2)}) async-start(), calls=%async_computation.5 | async-start | bytes 8650752 | tf_op jit(solution)/shard_map/reduce_scatter | solution.py:12
  129.2 19.0 %copy-start.1 = (s32[8,22]{1,0:T(8,128)S(1)}, s32[8,22]{1,0:T(8,128)}, u32[]{:S(2)}) copy-start(s32[8,22]{1,0:T(8,128)} %param.14) | copy-start | bytes 2116
  212.5 11.8 %copy-start.3 = (bf16[256,8192]{1,0:T(8,128)(2,1)S(1)}, bf16[256,8192]{1,0:T(8,128)(2,1)}, u32[]{:S(2)}) copy-start(bf16[256,8192]{1,0:T(8,128)(2,1)} %all-gather.6.cloned.1.call-done) | copy-start | bytes 12582916
  224.3 77.9 %copy-start.2 = (s32[8,22]{1,0:T(8,128)S(1)}, s32[8,22]{1,0:T(8,128)}, u32[]{:S(2)}) copy-start(s32[8,22]{1,0:T(8,128)} %param.16) | copy-start | bytes 2116
Sparse Core Ops, SparseCore 0:
  9.9 129.7 all-gather.3
  141.5 70.9 all-gather.5
  215.1 87.0 all-gather.7
  337.0 130.4 reduce-scatter.1
